TPU v7x, 32 devices: a whole 2x2x4 slice. The times are simulated.
32 devices in a mesh: replica: 4 (over z), row: 4 (over y, x), col: 2 (over core).
Axes of the slice: x: 2, y: 2, z: 4, core: 2. Of those that a mesh axis runs over, the one named last changes fastest.
Arguments:
- hidden: bfloat16 [4, 1408, 14336], P('replica', 'col', 'row'), may hold values from -6 to 6
- cotangent: bfloat16 [4, 1408, 4096], P('replica', 'row', 'col'), may hold values from -6 to 6
- weight: bfloat16 [4, 14336, 4096], P('replica', 'row', 'col'), may hold values from -6 to 6
- prev_weight: bfloat16 [4, 14336, 4096], P('replica', 'row', 'col'), may hold values from -6 to 6
- prev_grad: bfloat16 [4, 14336, 4096], P('replica', 'row', 'col'), may hold values from -3 to 3
Outputs:
- output: bfloat16 [4, 1408, 4096], P('replica', 'row', 'col')
- hidden_grad: bfloat16 [4, 1408, 14336], P('replica', 'col', 'row')
- new_weight: bfloat16 [4, 14336, 4096], P('replica', 'row', 'col')
All inputs are finite; a program needn't handle non-finite values.
Results may differ from a plain program's by a relative error of at most 0.017.
Values may be sent and summed in bfloat16 or wider, within the bound.
A program may use at most 192 MiB of HBM per device.

v0:
```python
import jax
import jax.numpy as jnp
from jax import lax
from jax.sharding import PartitionSpec as P

FF = 14336


def shifted(array, axis, by):
    peers = lax.axis_size(axis)
    return lax.ppermute(array, axis, [(i, (i + by) % peers) for i in range(peers)])


def neighbours(blend):
    left = shifted(blend, "replica", 1)
    right = shifted(blend, "replica", -1)
    return (left.astype(jnp.float32), right.astype(jnp.float32))


def on_device(hidden, cotangent, weight, prev_weight, prev_grad):
    scale = FF ** (-0.5)
    blend_low = (weight[0].astype(jnp.float32) - 0.5 * prev_weight[0].astype(jnp.float32)).astype(
        jnp.bfloat16
    )
    gathered = lax.all_gather(hidden[0], "col", axis=0, tiled=True)
    upstream = lax.all_gather(cotangent[0], "row", axis=0, tiled=True)
    matrix = weight[0]
    partial_value = jnp.dot(gathered, matrix, preferred_element_type=jnp.float32) * scale
    output = lax.psum_scatter(
        partial_value.astype(jnp.bfloat16), "row", scatter_dimension=0, tiled=True
    )
    term = (
        lax.dot_general(
            upstream, matrix, (((1,), (1,)), ((), ())), preferred_element_type=jnp.float32
        )
        * scale
    )
    hidden_grad = lax.psum_scatter(
        term.astype(jnp.bfloat16), "col", scatter_dimension=0, tiled=True
    )
    grad = (
        lax.dot_general(
            gathered, upstream, (((0,), (0,)), ((), ())), preferred_element_type=jnp.float32
        )
        * scale
    )
    left, right = neighbours(blend_low)
    blend = blend_low.astype(jnp.float32)
    fresh = blend + (left + blend + right) / 3.0 - 0.5 * (grad - prev_grad[0].astype(jnp.float32))
    return (output[None], hidden_grad[None], fresh.astype(jnp.bfloat16)[None])


def solution(mesh):
    placed = (
        P("replica", "col", "row"),
        P("replica", "row", "col"),
        P("replica", "row", "col"),
        P("replica", "row", "col"),
        P("replica", "row", "col"),
    )
    return jax.shard_map(
        on_device,
        mesh=mesh,
        in_specs=placed,
        out_specs=(
            P("replica", "row", "col"),
            P("replica", "col", "row"),
            P("replica", "row", "col"),
        ),
        check_vma=False,
    )
```

profile of v0, /device:TPU:0, one launch (start us, length us, event | category | flops | bytes accessed | tf_op | source)
XLA Modules:
  0.0 767.7 jit_solution(11719800618483480351)
XLA Ops:
  7.2 0.0 all-gather.5.cloned.1.call-start
  7.2 0.7 all-gather.5.cloned.1.call-update
  7.9 0.0 all-gather.7.cloned.1.call-start
  7.9 0.7 all-gather.7.cloned.1.call-update
  8.6 0.0 reduce-scatter.3.cloned.1.call-start
  8.7 25.9 %all-gather.5.cloned.1.call-done = bf16[1,1408,3584]{2,1,0:T(8,128)(2,1)} async-done(((bf16[1,704,3584]{2,1,0:T(8,128)(2,1)}), bf16[1,1408,3584]{2,1,0:T(8,128)(2,1)}) %all-gather.5.cloned.1.call-update) | async-done | bytes 10092560 | tf_op jit(solution)/shard_map/all_gather | solution.py:25
  34.6 27.8 %multiply_convert_fusion = bf16[1408,2048]{1,0:T(8,128)(2,1)} fusion(bf16[1,3584,2048]{2,1,0:T(8,128)(2,1)} %param.7, bf16[1,1408,3584]{2,1,0:T(8,128)(2,1)} %all-gather.5.cloned.1.call-done), kind=kOutput, calls=%fused_computation.16 | convolution fusion | flops 20675297280 | bytes 30539776 | tf_op jit(solution)/shard_map/dot_general | solution.py:28
  62.3 0.0 reduce-scatter.3.cloned.1.call-update
  62.4 0.0 reduce-scatter.5.cloned.1.call-start
  62.4 18.9 %fusion.5 = bf16[3584,2048]{1,0:T(8,128)(2,1)} fusion(bf16[1,3584,2048]{2,1,0:T(8,128)(2,1)} %param.8, bf16[1,3584,2048]{2,1,0:T(8,128)(2,1)} %param.7), kind=kLoop, calls=%fused_computation.9 | loop fusion | flops 36700160 | bytes 44040192 | tf_op jit(solution)/shard_map/convert_element_type | solution.py:22
  81.4 1.7 collective-permute-start
  83.1 2.1 collective-permute-start.1
  85.2 18.1 %all-gather.7.cloned.1.call-done = bf16[1,1408,2048]{2,1,0:T(8,128)(2,1)} async-done(((bf16[1,352,2048]{2,1,0:T(8,128)(2,1)}), bf16[1,1408,2048]{2,1,0:T(8,128)(2,1)}) %all-gather.7.cloned.1.call-update) | async-done | bytes 5767184 | tf_op jit(solution)/shard_map/all_gather | solution.py:26
  103.3 28.4 %fusion.6 = bf16[1408,3584]{1,0:T(8,128)(2,1)} fusion(bf16[1,3584,2048]{2,1,0:T(8,128)(2,1)} %param.7, bf16[1,1408,2048]{2,1,0:T(8,128)(2,1)} %all-gather.7.cloned.1.call-done), kind=kOutput, calls=%fused_computation.11 | convolution fusion | flops 20679622656 | bytes 30539776 | tf_op jit(solution)/shard_map/dot_general | solution.py:33
  131.7 0.0 reduce-scatter.5.cloned.1.call-update
  131.7 269.9 %collective-permute-done = bf16[3584,2048]{1,0:T(8,128)(2,1)} collective-permute-done((bf16[3584,2048]{1,0:T(8,128)(2,1)}, bf16[3584,2048]{1,0:T(8,128)(2,1)}, u32[]{:S(2)}, u32[]{:S(2)}) %collective-permute-start) | collective-permute-done | bytes 14680096 | tf_op jit(solution)/shard_map/ppermute | solution.py:11
  401.7 313.5 %collective-permute-done.1 = bf16[3584,2048]{1,0:T(8,128)(2,1)} collective-permute-done((bf16[3584,2048]{1,0:T(8,128)(2,1)}, bf16[3584,2048]{1,0:T(8,128)(2,1)}, u32[]{:S(2)}, u32[]{:S(2)}) %collective-permute-start.1) | collective-permute-done | bytes 14680096 | tf_op jit(solution)/shard_map/ppermute | solution.py:11
  715.2 46.0 %fusion.10 = bf16[1,3584,2048]{2,1,0:T(8,128)(2,1)} fusion(bf16[1,3584,2048]{2,1,0:T(8,128)(2,1)} %param.9, bf16[3584,2048]{1,0:T(8,128)(2,1)} %collective-permute-done.1, bf16[3584,2048]{1,0:T(8,128)(2,1)} %collective-permute-done, bf16[3584,2048]{1,0:T(8,128)(2,1)} %fusion.5, bf16[1,1408,3584]{2,1,0:T(8,128)(2,1)} %all-gather.5.cloned.1.call-done, ...), kind=kOutput, calls=%fused_computation.15 | convolution fusion | flops 20764950528 | bytes 89260032 | tf_op jit(solution)/shard_map/dot_general | solution.py:42
  761.2 0.0 reduce-scatter.3.cloned.1.call-done
  761.2 0.0 reduce-scatter.5.cloned.1.call-done
Async XLA Ops:
  7.2 27.4 %all-gather.5.cloned.1.call-start = ((), (), s32[]{:S(2)}) async-start(), calls=%async_computation.4 | async-start | bytes 15138816 | tf_op jit(solution)/shard_map/all_gather | solution.py:25
  7.9 95.4 %all-gather.7.cloned.1.call-start = ((), (), s32[]{:S(2)}) async-start(), calls=%async_computation.5 | async-start | bytes 7208960 | tf_op jit(solution)/shard_map/all_gather | solution.py:26
  8.6 752.5 %reduce-scatter.3.cloned.1.call-start = ((), (), s32[]{:S(2)}) async-start(), calls=%async_computation.2 | async-start | bytes 7208960 | tf_op jit(solution)/shard_map/reduce_scatter | solution.py:29
  62.4 698.8 %reduce-scatter.5.cloned.1.call-start = ((), (), s32[]{:S(2)}) async-start(), calls=%async_computation.3 | async-start | bytes 15138816 | tf_op jit(solution)/shard_map/reduce_scatter | solution.py:38
  81.4 320.3 %collective-permute-start = (bf16[3584,2048]{1,0:T(8,128)(2,1)}, bf16[3584,2048]{1,0:T(8,128)(2,1)}, u32[]{:S(2)}, u32[]{:S(2)}) collective-permute-start(bf16[3584,2048]{1,0:T(8,128)(2,1)} %fusion.5), channel_id=1, source_target_pairs={{0,8},{8,16},{16,24},{24,0},{1,9},{9,17},{17,25},{25,1},{2,10},{10... | collective-permute-start | bytes 44040200 | tf_op jit(solution)/shard_map/ppermute | solution.py:11
  83.1 632.1 %collective-permute-start.1 = (bf16[3584,2048]{1,0:T(8,128)(2,1)}, bf16[3584,2048]{1,0:T(8,128)(2,1)}, u32[]{:S(2)}, u32[]{:S(2)}) collective-permute-start(bf16[3584,2048]{1,0:T(8,128)(2,1)} %fusion.5), channel_id=1, source_target_pairs={{0,24},{8,0},{16,8},{24,16},{1,25},{9,1},{17,9},{25,17},{2,26},{10... | collective-permute-start | bytes 44040200 | tf_op jit(solution)/shard_map/ppermute | solution.py:11
Sparse Core Ops, SparseCore 0:
  9.5 24.9 all-gather.4
  36.4 66.8 all-gather.6
  106.8 65.6 reduce-scatter.2
  175.3 17.6 reduce-scatter.4
where the time goes:
time: 768 us
  waiting for transfers between devices  629 us (82%)
  matrix products  102 us (13%)
  other arithmetic  18.9 us (2%)
  between operations  13.8 us (2%)
    ppermute x2, waiting for transfers between devices, shifted(): lax.ppermute(array, axis, [(i, (i + by) % peers) for i in range(peers)])  583 us
    dot_general x1, matrix products, on_device(): lax.dot_general(gathered, upstream, (((0,), (0,)), ((), ())), preferred_e...  46 us
    dot_general x1, matrix products, on_device(): lax.dot_general(upstream, matrix, (((1,), (1,)), ((), ())), preferred_ele...  28.4 us
    dot_general x1, matrix products, on_device(): jnp.dot(gathered, matrix, preferred_element_type=jnp.float32) * scale  27.8 us
    all_gather x1, waiting for transfers between devices, on_device(): gathered = lax.all_gather(hidden[0], 'col', axis=0, tiled=True)  25.9 us
    convert_element_type x1, other arithmetic, on_device(): (weight[0].astype(jnp.float32) - 0.5 * prev_weight[0].astype(jnp.float32)...  18.9 us
    all_gather x1, waiting for transfers between devices, on_device(): upstream = lax.all_gather(cotangent[0], 'row', axis=0, tiled=True)  18.1 us
  transfers between devices with their start and end apart: 6, of which 4 were waited for; matrix products, arithmetic and copies ran while one was open for 16% of the time, Pallas kernels for 0%

commit v1 on v0

v1 whole, which is shorter than its diff:
```python
import jax
import jax.numpy as jnp
from jax import lax
from jax.sharding import PartitionSpec as P


FF = 14336
PARTS = (2, 22, 26, 5, 1)
DIRECT = 4


def shifted(array, axis, by):
    peers = lax.axis_size(axis)
    return lax.ppermute(array, axis, [(i, (i + by) % peers) for i in range(peers)])


def gather_rows(block, axis):
    peers = lax.axis_size(axis)
    if peers > DIRECT:
        return lax.all_gather(block, axis, axis=0, tiled=True)
    me, size = lax.axis_index(axis), block.shape[0]
    whole = jnp.zeros((peers * size, block.shape[1]), block.dtype)
    whole = lax.dynamic_update_slice(whole, block, (me * size, 0))
    for step in range(1, peers):
        other = shifted(block, axis, step)
        owner = lax.rem(me - step + peers, peers)
        whole = lax.dynamic_update_slice(whole, other, (owner * size, 0))
    return whole


def sum_rows(partial, axis):
    peers = lax.axis_size(axis)
    if peers > DIRECT:
        return lax.psum_scatter(partial, axis, scatter_dimension=0, tiled=True)
    me, size = lax.axis_index(axis), partial.shape[0] // peers

    def block(owner):
        return lax.dynamic_slice_in_dim(partial, owner * size, size, 0)

    total = block(me).astype(jnp.float32)
    for step in range(1, peers):
        total += shifted(block(lax.rem(me + step, peers)), axis, step).astype(jnp.float32)
    return total.astype(partial.dtype)


def row_chunks(rows):
    total = sum(PARTS)
    if rows % (16 * total):
        return [(0, rows)]
    unit, at, chunks = rows // total, 0, []
    for part in PARTS:
        chunks.append((at, part * unit))
        at += part * unit
    return chunks


def on_device(hidden, cotangent, weight, prev_weight, prev_grad):
    scale = FF ** (-0.5)
    matrix, before, slope = weight[0], prev_weight[0], prev_grad[0]
    rows = matrix.shape[0]
    chunks = row_chunks(rows)

    lefts, rights = [], []
    for at, size in chunks:
        piece = (
            matrix[at : at + size].astype(jnp.float32)
            - 0.5 * before[at : at + size].astype(jnp.float32)
        ).astype(jnp.bfloat16)
        lefts.append(shifted(piece, "replica", 1))
        rights.append(shifted(piece, "replica", -1))

    gathered = gather_rows(hidden[0], "col")
    upstream = gather_rows(cotangent[0], "row")
    partial_value = (
        jnp.dot(gathered, matrix, preferred_element_type=jnp.float32) * scale
    ).astype(jnp.bfloat16)
    output = sum_rows(partial_value, "row")
    term = (
        lax.dot_general(
            upstream, matrix, (((1,), (1,)), ((), ())), preferred_element_type=jnp.float32
        )
        * scale
    )
    hidden_grad = sum_rows(term.astype(jnp.bfloat16), "col")
    grad = (
        lax.dot_general(
            gathered, upstream, (((0,), (0,)), ((), ())), preferred_element_type=jnp.float32
        )
        * scale
    )
    own = (
        matrix.astype(jnp.float32) - 0.5 * before.astype(jnp.float32)
    ).astype(jnp.bfloat16).astype(jnp.float32)
    base = own * (4.0 / 3.0) - 0.5 * (grad - slope.astype(jnp.float32))
    base, output, hidden_grad = lax.optimization_barrier((base, output, hidden_grad))

    fresh = jnp.zeros(matrix.shape, jnp.bfloat16)
    for (at, size), left, right in zip(chunks, lefts, rights):
        around = (left.astype(jnp.float32) + right.astype(jnp.float32)) * (1.0 / 3.0)
        piece = (base[at : at + size] + around).astype(jnp.bfloat16)
        fresh = lax.dynamic_update_slice(fresh, piece, (at, 0))
    return (output[None], hidden_grad[None], fresh[None])


def solution(mesh):
    placed = (
        P("replica", "col", "row"),
        P("replica", "row", "col"),
        P("replica", "row", "col"),
        P("replica", "row", "col"),
        P("replica", "row", "col"),
    )
    return jax.shard_map(
        on_device,
        mesh=mesh,
        in_specs=placed,
        out_specs=(
            P("replica", "row", "col"),
            P("replica", "col", "row"),
            P("replica", "row", "col"),
        ),
        check_vma=False,
    )
```

time: 768 us -> 666 us (0.87)
  waiting for transfers between devices: 629 us -> 399 us
  starting transfers between devices: 3.98 us -> 61.4 us
  other arithmetic: 18.9 us -> 69.6 us
  local copies, waits for them, and re-layouts: 0 us -> 43.1 us
  between operations: 13.8 us -> 0.72 us
  matrix products: 102 us -> 91.8 us
    ppermute x2 -> x18, waiting for transfers between devices: 583 us -> 399 us  [shifted(): lax.ppermute(array, axis, [(i, (i + by) % peers) for i in range(peers)])]
    ppermute x2 -> x18, starting transfers between devices: 3.82 us -> 61.4 us  [shifted(): lax.ppermute(array, axis, [(i, (i + by) % peers) for i in range(peers)])]
    all_gather x2 -> x0, waiting for transfers between devices: 43.9 us -> none  [the longest x1 25.9 us: on_device(): gathered = lax.all_gather(hidden[0], 'col', axis=0, tiled=True)]
    dynamic_update_slice x0 -> x4, other arithmetic: none -> 28.3 us  [on_device(): fresh = lax.dynamic_update_slice(fresh, piece, (at, 0))]
    convert_element_type x1 -> x8, other arithmetic: 18.9 us -> 41.2 us  [the longest x5 27.9 us: on_device(): piece = (matrix[at:at + size].astype(jnp.float32) - 0.5 * before[at:at +...]
    dynamic_update_slice x0 -> x6, local copies, waits for them, and re-layouts: none -> 18 us  [the longest x4 11.6 us: gather_rows(): whole = lax.dynamic_update_slice(whole, other, (owner * size, 0))]
    broadcast_in_dim x0 -> x3, local copies, waits for them, and re-layouts: none -> 16 us  [the longest x2 8.66 us: gather_rows(): whole = jnp.zeros((peers * size, block.shape[1]), block.dtype)]
  transfers between devices with their start and end apart: 6 -> 18, of which waited for: 4 -> 7; matrix products, arithmetic and copies ran while one was open for 16% -> 30% of each run, Pallas kernels for 0% -> 0%
where the time goes in v1:
time: 666 us; the launch traced here: 665 us
  waiting for transfers between devices  399 us (60%)
  matrix products  91.8 us (14%)
  other arithmetic  69.6 us (10%)
  starting transfers between devices  61.4 us (9%)
  local copies, waits for them, and re-layouts  43.1 us (6%)
    ppermute x18, waiting for transfers between devices, shifted(): lax.ppermute(array, axis, [(i, (i + by) % peers) for i in range(peers)])  399 us
    ppermute x18, starting transfers between devices, shifted(): lax.ppermute(array, axis, [(i, (i + by) % peers) for i in range(peers)])  61.4 us
    dot_general x1, matrix products, on_device(): lax.dot_general(gathered, upstream, (((0,), (0,)), ((), ())), preferred_e...  41.9 us
    dynamic_update_slice x4, other arithmetic, on_device(): fresh = lax.dynamic_update_slice(fresh, piece, (at, 0))  28.3 us
    convert_element_type x5, other arithmetic, on_device(): piece = (matrix[at:at + size].astype(jnp.float32) - 0.5 * before[at:at +...  27.9 us
    dot_general x1, matrix products, on_device(): lax.dot_general(upstream, matrix, (((1,), (1,)), ((), ())), preferred_ele...  25.2 us
    dot_general x1, matrix products, on_device(): jnp.dot(gathered, matrix, preferred_element_type=jnp.float32) * scale  24.8 us
  transfers between devices with their start and end apart: 18, of which 7 were waited for; matrix products, arithmetic and copies ran while one was open for 30% of the time, Pallas kernels for 0%

profile of v1, /device:TPU:0, one launch (start us, length us, event | category | flops | bytes accessed | tf_op | source)
XLA Modules:
  0.0 665.1 jit_solution(7248940568178509766)
XLA Ops:
  0.6 3.0 collective-permute-start.1
  3.6 1.5 collective-permute-start.2
  5.2 1.4 collective-permute-start.3
  6.6 2.2 fusion.18
  8.8 3.6 collective-permute-start.9
  12.4 8.8 %fusion.12 = bf16[1408,2048]{1,0:T(8,128)(2,1)} fusion(bf16[1,3584,2048]{2,1,0:T(8,128)(2,1)} %param.8, bf16[1,3584,2048]{2,1,0:T(8,128)(2,1)} %param.7), kind=kLoop, calls=%fused_computation.20 | loop fusion | flops 14417920 | bytes 17301504 | tf_op jit(solution)/shard_map/convert_element_type | solution.py:68
  21.2 3.2 broadcast_in_dim.25
  24.4 1.2 constant_dynamic-update-slice_fusion.3
  25.6 5.5 broadcast_in_dim.24
  31.1 5.2 constant_dynamic-update-slice_fusion.5
  36.3 1.1 collective-permute-done.1
  37.4 4.1 collective-permute-start.11
  41.5 2.6 constant_dynamic-update-slice_fusion.2
  44.1 23.3 %collective-permute-done.2 = bf16[352,2048]{1,0:T(8,128)(2,1)} collective-permute-done((bf16[352,2048]{1,0:T(8,128)(2,1)}, bf16[352,2048]{1,0:T(8,128)(2,1)}, u32[]{:S(2)}, u32[]{:S(2)}) %collective-permute-start.2) | collective-permute-done | bytes 1441824 | tf_op jit(solution)/shard_map/ppermute | solution.py:14
  67.4 2.6 constant_dynamic-update-slice_fusion.1
  70.0 1.2 constant_dynamic-update-slice_fusion
  71.3 25.2 %fusion.3 = bf16[1408,3584]{1,0:T(8,128)(2,1)} fusion(bf16[1408,2048]{1,0:T(8,128)(2,1)} %constant_dynamic-update-slice_fusion, bf16[1,3584,2048]{2,1,0:T(8,128)(2,1)S(1)} %bitcast.56), kind=kOutput, calls=%fused_computation.6 | convolution fusion | flops 20679622656 | bytes 30539776 | tf_op jit(solution)/shard_map/dot_general | solution.py:79
  96.5 5.0 constant_dynamic-slice_fusion
  101.5 0.0 collective-permute-start.7
  101.5 5.0 constant_dynamic-update-slice_fusion.4
  106.6 24.8 %multiply_convert_fusion = bf16[1408,2048]{1,0:T(8,128)(2,1)S(1)} fusion(bf16[1408,3584]{1,0:T(8,128)(2,1)} %constant_dynamic-update-slice_fusion.4, bf16[1,3584,2048]{2,1,0:T(8,128)(2,1)S(1)} %bitcast.56), kind=kOutput, calls=%fused_computation.15 | convolution fusion | flops 20675297280 | bytes 30539776 | tf_op jit(solution)/shard_map/dot_general | solution.py:75
  131.4 2.5 copy-done
  133.9 1.5 constant_dynamic-slice_fusion.3
  135.4 1.8 collective-permute-start.6
  137.2 1.6 collective-permute-start.5
  138.8 11.8 %fusion.9 = bf16[1664,2048]{1,0:T(8,128)(2,1)} fusion(bf16[1,3584,2048]{2,1,0:T(8,128)(2,1)} %param.8, bf16[1,3584,2048]{2,1,0:T(8,128)(2,1)} %param.7), kind=kLoop, calls=%fused_computation.17 | loop fusion | flops 17039360 | bytes 20447232 | tf_op jit(solution)/shard_map/convert_element_type | solution.py:68
  150.6 1.8 fusion.19
  152.4 3.3 fusion.15
  155.7 1.6 collective-permute-start.10
  157.3 12.6 %collective-permute-done.6 = bf16[352,2048]{1,0:T(8,128)(2,1)} collective-permute-done((bf16[352,2048]{1,0:T(8,128)(2,1)}, bf16[352,2048]{1,0:T(8,128)(2,1)}, u32[]{:S(2)}, u32[]{:S(2)}) %collective-permute-start.6) | collective-permute-done | bytes 1441824 | tf_op jit(solution)/shard_map/ppermute | solution.py:14
  169.9 3.6 collective-permute-start.13
  173.5 30.4 %collective-permute-start.4 = (bf16[352,2048]{1,0:T(8,128)(2,1)S(1)}, bf16[352,2048]{1,0:T(8,128)(2,1)S(1)}, u32[]{:S(2)}, u32[]{:S(2)}) collective-permute-start(bf16[352,2048]{1,0:T(8,128)(2,1)S(1)} %get-tuple-element.9), channel_id=1, source_target_pairs={{0,2},{2,4},{4,6},{6,0},{1,3},{3,5},{5,7},{7,1},{8,10},{10,12},{12... | collective-permute-start | bytes 4325384 | tf_op jit(solution)/shard_map/ppermute | solution.py:14
  203.9 41.9 %fusion.1 = f32[3584,2048]{1,0:T(8,128)} fusion(bf16[1408,3584]{1,0:T(8,128)(2,1)} %constant_dynamic-update-slice_fusion.4, bf16[1408,2048]{1,0:T(8,128)(2,1)} %constant_dynamic-update-slice_fusion, bf16[1,3584,2048]{2,1,0:T(8,128)(2,1)} %param.8, bf16[1,3584,2048]{2,1,0:T(8,128)(2,1)} %param.9, bf16[1,3584,2048]{2,1,0:T(8,128)(2,1)} %param.7), kind=kOutput, calls=%fused_computation.2 | convolution fusion | flops 20757610496 | bytes 89260032 | tf_op jit(solution)/shard_map/dot_general | solution.py:86
  245.8 7.5 %add_convert_fusion.2 = bf16[704,3584]{1,0:T(8,128)(2,1)} fusion(bf16[704,3584]{1,0:T(8,128)(2,1)} %collective-permute-done.7, bf16[1408,3584]{1,0:T(8,128)(2,1)} %fusion.3, s32[]{:T(128)S(6)} %select_n.24), kind=kLoop, calls=%fused_computation.16 | loop fusion | flops 10092544 | bytes 15138820 | tf_op jit(solution)/shard_map/convert_element_type | solution.py:43
  253.3 1.6 collective-permute-start.8
  254.9 4.4 add_convert_fusion.3
  259.3 331.8 %collective-permute-done.8 = bf16[128,2048]{1,0:T(8,128)(2,1)S(1)} collective-permute-done((bf16[128,2048]{1,0:T(8,128)(2,1)}, bf16[128,2048]{1,0:T(8,128)(2,1)S(1)}, u32[]{:S(2)}, u32[]{:S(2)}) %collective-permute-start.8) | collective-permute-done | bytes 524320 | tf_op jit(solution)/shard_map/ppermute | solution.py:14
  591.1 3.3 collective-permute-start.15
  594.5 1.4 add_convert_fusion.5
  595.9 7.3 %pad_bitcast_fusion = bf16[1,3584,2048]{2,1,0:T(8,128)(2,1)} fusion(bf16[128,2048]{1,0:T(8,128)(2,1)S(1)} %add_convert_fusion.5), kind=kLoop, calls=%fused_computation.10 | loop fusion | bytes 15204352 | tf_op jit(solution)/shard_map/broadcast_in_dim | solution.py:102
  603.3 3.8 collective-permute-start.17
  607.1 10.8 %fusion.14 = bf16[1,3584,2048]{2,1,0:T(8,128)(2,1)} fusion(bf16[1,3584,2048]{2,1,0:T(8,128)(2,1)} %pad_bitcast_fusion, bf16[1408,2048]{1,0:T(8,128)(2,1)} %collective-permute-done.11, bf16[1408,2048]{1,0:T(8,128)(2,1)} %collective-permute-done.10, f32[3584,2048]{1,0:T(8,128)} %fusion.1), kind=kLoop, calls=%fused_computation.22 | loop fusion | flops 17301504 | bytes 28835840 | tf_op jit(solution)/shard_map/dynamic_update_slice | solution.py:101
  617.9 12.3 %fusion.11 = bf16[1,3584,2048]{2,1,0:T(8,128)(2,1)} fusion(bf16[1,3584,2048]{2,1,0:T(8,128)(2,1)} %fusion.14, bf16[1664,2048]{1,0:T(8,128)(2,1)} %collective-permute-done.13, bf16[1664,2048]{1,0:T(8,128)(2,1)} %collective-permute-done.12, f32[3584,2048]{1,0:T(8,128)} %fusion.1), kind=kLoop, calls=%fused_computation.19 | loop fusion | flops 20447232 | bytes 34078720 | tf_op jit(solution)/shard_map/dynamic_update_slice | solution.py:101
  630.2 22.8 %collective-permute-done.14 = bf16[320,2048]{1,0:T(8,128)(2,1)S(1)} collective-permute-done((bf16[320,2048]{1,0:T(8,128)(2,1)}, bf16[320,2048]{1,0:T(8,128)(2,1)S(1)}, u32[]{:S(2)}, u32[]{:S(2)}) %collective-permute-start.14) | collective-permute-done | bytes 1310752 | tf_op jit(solution)/shard_map/ppermute | solution.py:14
  653.0 3.4 fusion.17
  656.4 1.2 collective-permute-done.17
  657.6 5.6 collective-permute-done.16
  663.3 1.8 fusion.21
  (29 shorter events, 0.1 us)
Async XLA Ops:
  0.6 36.8 %collective-permute-start.1 = (bf16[352,2048]{1,0:T(8,128)(2,1)}, bf16[352,2048]{1,0:T(8,128)(2,1)}, u32[]{:S(2)}, u32[]{:S(2)}) collective-permute-start(bf16[352,2048]{1,0:T(8,128)(2,1)} %bitcast.60), channel_id=1, source_target_pairs={{0,2},{2,4},{4,6},{6,0},{1,3},{3,5},{5,7},{7,1},{8,10},{10,12},{12... | collective-permute-start | bytes 4325384 | tf_op jit(solution)/shard_map/ppermute | solution.py:14
  3.6 63.8 %collective-permute-start.2 = (bf16[352,2048]{1,0:T(8,128)(2,1)}, bf16[352,2048]{1,0:T(8,128)(2,1)}, u32[]{:S(2)}, u32[]{:S(2)}) collective-permute-start(bf16[352,2048]{1,0:T(8,128)(2,1)} %bitcast.61), channel_id=1, source_target_pairs={{0,4},{2,6},{4,0},{6,2},{1,5},{3,7},{5,1},{7,3},{8,12},{10,14},{12... | collective-permute-start | bytes 4325384 | tf_op jit(solution)/shard_map/ppermute | solution.py:14
  5.2 64.9 %collective-permute-start.3 = (bf16[352,2048]{1,0:T(8,128)(2,1)}, bf16[352,2048]{1,0:T(8,128)(2,1)S(1)}, u32[]{:S(2)}, u32[]{:S(2)}) collective-permute-start(bf16[352,2048]{1,0:T(8,128)(2,1)} %bitcast.62), channel_id=1, source_target_pairs={{0,6},{2,0},{4,2},{6,4},{1,7},{3,1},{5,3},{7,5},{8,14},{10,8},{12,... | collective-permute-start | bytes 4325384 | tf_op jit(solution)/shard_map/ppermute | solution.py:14
  6.6 94.9 %collective-permute-start = (bf16[704,3584]{1,0:T(8,128)(2,1)}, bf16[704,3584]{1,0:T(8,128)(2,1)}, u32[]{:S(2)}, u32[]{:S(2)}) collective-permute-start(bf16[704,3584]{1,0:T(8,128)(2,1)} %bitcast.57), channel_id=1, source_target_pairs={{0,1},{1,0},{2,3},{3,2},{4,5},{5,4},{6,7},{7,6},{8,9},{9,8},{10,11... | collective-permute-start | bytes 15138824 | tf_op jit(solution)/shard_map/ppermute | solution.py:14
  8.8 146.9 %collective-permute-start.9 = (bf16[128,2048]{1,0:T(8,128)(2,1)}, bf16[128,2048]{1,0:T(8,128)(2,1)S(1)}, u32[]{:S(2)}, u32[]{:S(2)}) collective-permute-start(bf16[128,2048]{1,0:T(8,128)(2,1)} %fusion.18), channel_id=1, source_target_pairs={{0,24},{8,0},{16,8},{24,16},{1,25},{9,1},{17,9},{25,17},{2,26},{10... | collective-permute-start | bytes 1572872 | tf_op jit(solution)/shard_map/ppermute | solution.py:14
  12.4 12.0 %copy-start.1 = (bf16[1,352,2048]{2,1,0:T(8,128)(2,1)S(1)}, bf16[1,352,2048]{2,1,0:T(8,128)(2,1)}, u32[]{:S(2)}) copy-start(bf16[1,352,2048]{2,1,0:T(8,128)(2,1)} %param.6) | copy-start | bytes 4325380
  25.6 45.7 %slice-start = ((s8[14680064]{0:T(1024)(128)(4,1)}), s8[4194304]{0:T(1024)(128)(4,1)S(1)}, s32[]{:S(2)}) async-start(s8[14680064]{0:T(1024)(128)(4,1)} %bitcast.55), calls=%async_computation | async-start | bytes 8388608
  25.6 45.7 %slice-start.1 = ((s8[14680064]{0:T(1024)(128)(4,1)}), s8[2097152]{0:T(1024)(128)(4,1)S(1)}, s32[]{:S(2)}) async-start(s8[14680064]{0:T(1024)(128)(4,1)} %bitcast.55), calls=%async_computation.1 | async-start | bytes 4194304
  31.1 40.2 %slice-start.2 = ((s8[14680064]{0:T(1024)(128)(4,1)}), s8[4194304]{0:T(1024)(128)(4,1)S(1)}, s32[]{:S(2)}) async-start(s8[14680064]{0:T(1024)(128)(4,1)} %bitcast.55), calls=%async_computation.2 | async-start | bytes 8388608
  36.3 35.0 %slice-start.3 = ((s8[14680064]{0:T(1024)(128)(4,1)}), s8[4194304]{0:T(1024)(128)(4,1)S(1)}, s32[]{:S(2)}) async-start(s8[14680064]{0:T(1024)(128)(4,1)} %bitcast.55), calls=%async_computation.3 | async-start | bytes 8388608
  37.4 565.8 %collective-permute-start.11 = (bf16[1408,2048]{1,0:T(8,128)(2,1)}, bf16[1408,2048]{1,0:T(8,128)(2,1)}, u32[]{:S(2)}, u32[]{:S(2)}) collective-permute-start(bf16[1408,2048]{1,0:T(8,128)(2,1)} %fusion.12), channel_id=1, source_target_pairs={{0,24},{8,0},{16,8},{24,16},{1,25},{9,1},{17,9},{25,17},{2,26},{10... | collective-permute-start | bytes 17301512 | tf_op jit(solution)/shard_map/ppermute | solution.py:14
  101.5 72.0 %collective-permute-start.7 = (bf16[704,3584]{1,0:T(8,128)(2,1)}, bf16[704,3584]{1,0:T(8,128)(2,1)}, u32[]{:S(2)}, u32[]{:S(2)}) collective-permute-start(bf16[704,3584]{1,0:T(8,128)(2,1)} %constant_dynamic-slice_fusion), channel_id=1, source_target_pairs={{0,1},{1,0},{2,3},{3,2},{4,5},{5,4},{6,7},{7,6},{8,9},{9,8},{10,11... | collective-permute-start | bytes 15138824 | tf_op jit(solution)/shard_map/ppermute | solution.py:14
  131.4 2.5 copy-start
  135.4 34.5 %collective-permute-start.6 = (bf16[352,2048]{1,0:T(8,128)(2,1)}, bf16[352,2048]{1,0:T(8,128)(2,1)}, u32[]{:S(2)}, u32[]{:S(2)}) collective-permute-start(bf16[352,2048]{1,0:T(8,128)(2,1)} %get-tuple-element.10), channel_id=1, source_target_pairs={{0,6},{2,0},{4,2},{6,4},{1,7},{3,1},{5,3},{7,5},{8,14},{10,8},{12,... | collective-permute-start | bytes 4325384 | tf_op jit(solution)/shard_map/ppermute | solution.py:14
  137.2 36.3 %collective-permute-start.5 = (bf16[352,2048]{1,0:T(8,128)(2,1)S(1)}, bf16[352,2048]{1,0:T(8,128)(2,1)}, u32[]{:S(2)}, u32[]{:S(2)}) collective-permute-start(bf16[352,2048]{1,0:T(8,128)(2,1)S(1)} %get-tuple-element.11), channel_id=1, source_target_pairs={{0,4},{2,6},{4,0},{6,2},{1,5},{3,7},{5,1},{7,3},{8,12},{10,14},{12... | collective-permute-start | bytes 4325384 | tf_op jit(solution)/shard_map/ppermute | solution.py:14
  155.7 447.5 %collective-permute-start.10 = (bf16[1408,2048]{1,0:T(8,128)(2,1)}, bf16[1408,2048]{1,0:T(8,128)(2,1)}, u32[]{:S(2)}, u32[]{:S(2)}) collective-permute-start(bf16[1408,2048]{1,0:T(8,128)(2,1)} %fusion.12), channel_id=1, source_target_pairs={{0,8},{8,16},{16,24},{24,0},{1,9},{9,17},{17,25},{25,1},{2,10},{10... | collective-permute-start | bytes 17301512 | tf_op jit(solution)/shard_map/ppermute | solution.py:14
  169.9 447.9 %collective-permute-start.13 = (bf16[1664,2048]{1,0:T(8,128)(2,1)}, bf16[1664,2048]{1,0:T(8,128)(2,1)}, u32[]{:S(2)}, u32[]{:S(2)}) collective-permute-start(bf16[1664,2048]{1,0:T(8,128)(2,1)} %fusion.9), channel_id=1, source_target_pairs={{0,24},{8,0},{16,8},{24,16},{1,25},{9,1},{17,9},{25,17},{2,26},{10... | collective-permute-start | bytes 20447240 | tf_op jit(solution)/shard_map/ppermute | solution.py:14
  173.5 444.3 %collective-permute-start.12 = (bf16[1664,2048]{1,0:T(8,128)(2,1)}, bf16[1664,2048]{1,0:T(8,128)(2,1)}, u32[]{:S(2)}, u32[]{:S(2)}) collective-permute-start(bf16[1664,2048]{1,0:T(8,128)(2,1)} %fusion.9), channel_id=1, source_target_pairs={{0,8},{8,16},{16,24},{24,0},{1,9},{9,17},{17,25},{25,1},{2,10},{10... | collective-permute-start | bytes 20447240 | tf_op jit(solution)/shard_map/ppermute | solution.py:14
  173.5 79.8 %collective-permute-start.4 = (bf16[352,2048]{1,0:T(8,128)(2,1)S(1)}, bf16[352,2048]{1,0:T(8,128)(2,1)S(1)}, u32[]{:S(2)}, u32[]{:S(2)}) collective-permute-start(bf16[352,2048]{1,0:T(8,128)(2,1)S(1)} %get-tuple-element.9), channel_id=1, source_target_pairs={{0,2},{2,4},{4,6},{6,0},{1,3},{3,5},{5,7},{7,1},{8,10},{10,12},{12... | collective-permute-start | bytes 4325384 | tf_op jit(solution)/shard_map/ppermute | solution.py:14
  253.3 337.8 %collective-permute-start.8 = (bf16[128,2048]{1,0:T(8,128)(2,1)}, bf16[128,2048]{1,0:T(8,128)(2,1)S(1)}, u32[]{:S(2)}, u32[]{:S(2)}) collective-permute-start(bf16[128,2048]{1,0:T(8,128)(2,1)} %fusion.18), channel_id=1, source_target_pairs={{0,8},{8,16},{16,24},{24,0},{1,9},{9,17},{17,25},{25,1},{2,10},{10... | collective-permute-start | bytes 1572872 | tf_op jit(solution)/shard_map/ppermute | solution.py:14
  259.3 343.9 %copy-start.2 = (bf16[64,2048]{1,0:T(8,128)(2,1)S(1)}, bf16[64,2048]{1,0:T(8,128)(2,1)}, u32[]{:S(2)}) copy-start(bf16[64,2048]{1,0:T(8,128)(2,1)} %fusion.19) | copy-start | bytes 786436
  591.1 39.0 %collective-permute-start.15 = (bf16[320,2048]{1,0:T(8,128)(2,1)}, bf16[320,2048]{1,0:T(8,128)(2,1)S(1)}, u32[]{:S(2)}, u32[]{:S(2)}) collective-permute-start(bf16[320,2048]{1,0:T(8,128)(2,1)} %fusion.15), channel_id=1, source_target_pairs={{0,24},{8,0},{16,8},{24,16},{1,25},{9,1},{17,9},{25,17},{2,26},{10... | collective-permute-start | bytes 3932168 | tf_op jit(solution)/shard_map/ppermute | solution.py:14
  603.2 49.8 %collective-permute-start.14 = (bf16[320,2048]{1,0:T(8,128)(2,1)}, bf16[320,2048]{1,0:T(8,128)(2,1)S(1)}, u32[]{:S(2)}, u32[]{:S(2)}) collective-permute-start(bf16[320,2048]{1,0:T(8,128)(2,1)} %fusion.15), channel_id=1, source_target_pairs={{0,8},{8,16},{16,24},{24,0},{1,9},{9,17},{17,25},{25,1},{2,10},{10... | collective-permute-start | bytes 3932168 | tf_op jit(solution)/shard_map/ppermute | solution.py:14
  603.3 54.4 %collective-permute-start.17 = (bf16[64,2048]{1,0:T(8,128)(2,1)S(1)}, bf16[64,2048]{1,0:T(8,128)(2,1)S(1)}, u32[]{:S(2)}, u32[]{:S(2)}) collective-permute-start(bf16[64,2048]{1,0:T(8,128)(2,1)S(1)} %copy-done.2), channel_id=1, source_target_pairs={{0,24},{8,0},{16,8},{24,16},{1,25},{9,1},{17,9},{25,17},{2,26},{10... | collective-permute-start | bytes 786440 | tf_op jit(solution)/shard_map/ppermute | solution.py:14
  617.8 45.4 %collective-permute-start.16 = (bf16[64,2048]{1,0:T(8,128)(2,1)S(1)}, bf16[64,2048]{1,0:T(8,128)(2,1)S(1)}, u32[]{:S(2)}, u32[]{:S(2)}) collective-permute-start(bf16[64,2048]{1,0:T(8,128)(2,1)S(1)} %copy-done.2), channel_id=1, source_target_pairs={{0,8},{8,16},{16,24},{24,0},{1,9},{9,17},{17,25},{25,1},{2,10},{10... | collective-permute-start | bytes 786440 | tf_op jit(solution)/shard_map/ppermute | solution.py:14

commit v2 on v1

--- a/solution.py
+++ b/solution.py
@@ -5,7 +5,7 @@
 
 
 FF = 14336
-PARTS = (2, 22, 26, 5, 1)
+PARTS = (1, 7, 20, 23, 4.5, 0.5)
 DIRECT = 4
 
 
@@ -44,13 +44,16 @@
 
 
 def row_chunks(rows):
-    total = sum(PARTS)
+    total = int(sum(PARTS))
     if rows % (16 * total):
         return [(0, rows)]
-    unit, at, chunks = rows // total, 0, []
-    for part in PARTS:
+    unit, at, chunks = int(rows // total), 0, []
+    for part in PARTS[:-2]:
         chunks.append((at, part * unit))
         at += part * unit
+    last = max(16, unit // 2)
+    chunks.append((at, rows - last - at))
+    chunks.append((rows - last, last))
     return chunks
 
 

time: 666 us -> 697 us (1.047)
  waiting for transfers between devices: 399 us -> 455 us
  starting transfers between devices: 61.4 us -> 29.5 us
  other arithmetic: 69.6 us -> 77.6 us
    ppermute x18 -> x20, waiting for transfers between devices: 399 us -> 455 us  [shifted(): lax.ppermute(array, axis, [(i, (i + by) % peers) for i in range(peers)])]
    ppermute x18 -> x20, starting transfers between devices: 61.4 us -> 29.5 us  [shifted(): lax.ppermute(array, axis, [(i, (i + by) % peers) for i in range(peers)])]
    dynamic_update_slice x4 -> x5, other arithmetic: 28.3 us -> 33.9 us  [on_device(): fresh = lax.dynamic_update_slice(fresh, piece, (at, 0))]
    convert_element_type x5 -> x6, other arithmetic: 27.9 us -> 30.4 us  [on_device(): piece = (matrix[at:at + size].astype(jnp.float32) - 0.5 * before[at:at +...]
  transfers between devices with their start and end apart: 18 -> 20, of which waited for: 7 -> 5; matrix products, arithmetic and copies ran while one was open for 30% -> 30% of each run, Pallas kernels for 0% -> 0%
where the time goes in v2:
time: 697 us
  waiting for transfers between devices  455 us (65%)
  matrix products  91.8 us (13%)
  other arithmetic  77.6 us (11%)
  local copies, waits for them, and re-layouts  42.5 us (6%)
  starting transfers between devices  29.5 us (4%)
    ppermute x20, waiting for transfers between devices, shifted(): lax.ppermute(array, axis, [(i, (i + by) % peers) for i in range(peers)])  455 us
    dot_general x1, matrix products, on_device(): lax.dot_general(gathered, upstream, (((0,), (0,)), ((), ())), preferred_e...  41.9 us
    dynamic_update_slice x5, other arithmetic, on_device(): fresh = lax.dynamic_update_slice(fresh, piece, (at, 0))  33.9 us
    convert_element_type x6, other arithmetic, on_device(): piece = (matrix[at:at + size].astype(jnp.float32) - 0.5 * before[at:at +...  30.4 us
    ppermute x20, starting transfers between devices, shifted(): lax.ppermute(array, axis, [(i, (i + by) % peers) for i in range(peers)])  29.5 us
    dot_general x1, matrix products, on_device(): lax.dot_general(upstream, matrix, (((1,), (1,)), ((), ())), preferred_ele...  25.1 us
    dot_general x1, matrix products, on_device(): jnp.dot(gathered, matrix, preferred_element_type=jnp.float32) * scale  24.8 us
  transfers between devices with their start and end apart: 20, of which 5 were waited for; matrix products, arithmetic and copies ran while one was open for 30% of the time, Pallas kernels for 0%

profile of v2, /device:TPU:0, one launch (start us, length us, event | category | flops | bytes accessed | tf_op | source)
XLA Modules:
  0.0 696.6 jit_solution(12946571513592155751)
XLA Ops:
  0.6 3.0 collective-permute-start.1
  3.6 1.5 collective-permute-start.2
  5.2 1.4 collective-permute-start.3
  6.6 1.8 fusion.21
  8.4 3.6 collective-permute-start.9
  12.0 4.1 fusion.15
  16.2 3.3 fusion.18
  19.5 3.2 broadcast_in_dim.27
  22.7 1.3 constant_dynamic-update-slice_fusion.3
  24.0 9.6 %fusion.12 = bf16[1280,2048]{1,0:T(8,128)(2,1)} fusion(bf16[1,3584,2048]{2,1,0:T(8,128)(2,1)} %param.8, bf16[1,3584,2048]{2,1,0:T(8,128)(2,1)} %param.7), kind=kLoop, calls=%fused_computation.20 | loop fusion | flops 13107200 | bytes 15728640 | tf_op jit(solution)/shard_map/convert_element_type | solution.py:71
  33.6 10.0 %fusion.9 = bf16[1472,2048]{1,0:T(8,128)(2,1)} fusion(bf16[1,3584,2048]{2,1,0:T(8,128)(2,1)} %param.8, bf16[1,3584,2048]{2,1,0:T(8,128)(2,1)} %param.7), kind=kLoop, calls=%fused_computation.17 | loop fusion | flops 15073280 | bytes 18087936 | tf_op jit(solution)/shard_map/convert_element_type | solution.py:71
  43.6 1.6 fusion.22
  45.2 4.6 broadcast_in_dim.26
  49.8 5.0 constant_dynamic-update-slice_fusion.5
  54.9 2.6 constant_dynamic-update-slice_fusion.2
  57.5 9.9 %collective-permute-done.2 = bf16[352,2048]{1,0:T(8,128)(2,1)} collective-permute-done((bf16[352,2048]{1,0:T(8,128)(2,1)}, bf16[352,2048]{1,0:T(8,128)(2,1)}, u32[]{:S(2)}, u32[]{:S(2)}) %collective-permute-start.2) | collective-permute-done | bytes 1441824 | tf_op jit(solution)/shard_map/ppermute | solution.py:14
  67.4 3.8 collective-permute-start.11
  71.2 2.6 constant_dynamic-update-slice_fusion.1
  73.8 0.5 collective-permute-start.13
  74.3 2.6 constant_dynamic-update-slice_fusion
  76.9 5.0 constant_dynamic-update-slice_fusion.4
  81.9 24.8 %multiply_convert_fusion = bf16[1408,2048]{1,0:T(8,128)(2,1)S(1)} fusion(bf16[1408,3584]{1,0:T(8,128)(2,1)} %constant_dynamic-update-slice_fusion.4, bf16[1,3584,2048]{2,1,0:T(8,128)(2,1)S(1)} %bitcast.62), kind=kOutput, calls=%fused_computation.13 | convolution fusion | flops 20675297280 | bytes 30539776 | tf_op jit(solution)/shard_map/dot_general | solution.py:78
  106.7 2.5 copy-done
  109.2 1.7 constant_dynamic-slice_fusion.3
  110.9 1.8 collective-permute-start.6
  112.7 25.1 %fusion.3 = bf16[1408,3584]{1,0:T(8,128)(2,1)} fusion(bf16[1408,2048]{1,0:T(8,128)(2,1)} %constant_dynamic-update-slice_fusion, bf16[1,3584,2048]{2,1,0:T(8,128)(2,1)S(1)} %bitcast.62), kind=kOutput, calls=%fused_computation.6 | convolution fusion | flops 20679622656 | bytes 30539776 | tf_op jit(solution)/shard_map/dot_general | solution.py:82
  137.8 2.8 constant_dynamic-slice_fusion
  140.6 1.6 collective-permute-start.12
  142.2 1.6 collective-permute-start.5
  143.9 1.1 copy-done.1
  145.0 1.3 collective-permute-start.4
  146.3 41.9 %fusion.1 = f32[3584,2048]{1,0:T(8,128)} fusion(bf16[1408,3584]{1,0:T(8,128)(2,1)} %constant_dynamic-update-slice_fusion.4, bf16[1408,2048]{1,0:T(8,128)(2,1)} %constant_dynamic-update-slice_fusion, bf16[1,3584,2048]{2,1,0:T(8,128)(2,1)} %param.8, bf16[1,3584,2048]{2,1,0:T(8,128)(2,1)} %param.9, bf16[1,3584,2048]{2,1,0:T(8,128)(2,1)} %param.7), kind=kOutput, calls=%fused_computation.2 | convolution fusion | flops 20757610496 | bytes 89260032 | tf_op jit(solution)/shard_map/dot_general | solution.py:89
  188.2 19.3 %collective-permute-done.5 = bf16[352,2048]{1,0:T(8,128)(2,1)} collective-permute-done((bf16[352,2048]{1,0:T(8,128)(2,1)}, bf16[352,2048]{1,0:T(8,128)(2,1)}, u32[]{:S(2)}, u32[]{:S(2)}) %collective-permute-start.5) | collective-permute-done | bytes 1441824 | tf_op jit(solution)/shard_map/ppermute | solution.py:14
  207.4 2.2 collective-permute-start.15
  209.7 7.5 %add_convert_fusion.2 = bf16[704,3584]{1,0:T(8,128)(2,1)} fusion(bf16[704,3584]{1,0:T(8,128)(2,1)} %collective-permute-done.7, bf16[1408,3584]{1,0:T(8,128)(2,1)} %fusion.3, s32[]{:T(128)S(6)} %select_n.24), kind=kLoop, calls=%fused_computation.16 | loop fusion | flops 10092544 | bytes 15138820 | tf_op jit(solution)/shard_map/convert_element_type | solution.py:43
  217.3 4.5 add_convert_fusion.4
  221.7 1.2 add_convert_fusion.6
  223.0 7.3 %pad_bitcast_fusion = bf16[1,3584,2048]{2,1,0:T(8,128)(2,1)} fusion(bf16[64,2048]{1,0:T(8,128)(2,1)S(1)} %add_convert_fusion.6), kind=kLoop, calls=%fused_computation.10 | loop fusion | bytes 14942208 | tf_op jit(solution)/shard_map/broadcast_in_dim | solution.py:105
  230.3 404.0 %collective-permute-done.10 = bf16[448,2048]{1,0:T(8,128)(2,1)S(1)} collective-permute-done((bf16[448,2048]{1,0:T(8,128)(2,1)}, bf16[448,2048]{1,0:T(8,128)(2,1)S(1)}, u32[]{:S(2)}, u32[]{:S(2)}) %collective-permute-start.10) | collective-permute-done | bytes 1835040 | tf_op jit(solution)/shard_map/ppermute | solution.py:14
  634.3 3.3 collective-permute-start.17
  637.6 4.7 fusion.17
  642.3 3.8 collective-permute-start.19
  646.1 12.8 %fusion.14 = bf16[1,3584,2048]{2,1,0:T(8,128)(2,1)} fusion(bf16[1,3584,2048]{2,1,0:T(8,128)(2,1)} %fusion.17, bf16[1280,2048]{1,0:T(8,128)(2,1)} %collective-permute-done.13, bf16[1280,2048]{1,0:T(8,128)(2,1)} %collective-permute-done.12, f32[3584,2048]{1,0:T(8,128)} %fusion.1), kind=kLoop, calls=%fused_computation.22 | loop fusion | flops 15728640 | bytes 26214400 | tf_op jit(solution)/shard_map/dynamic_update_slice | solution.py:104
  659.0 11.1 %fusion.11 = bf16[1,3584,2048]{2,1,0:T(8,128)(2,1)} fusion(bf16[1,3584,2048]{2,1,0:T(8,128)(2,1)} %fusion.14, bf16[1472,2048]{1,0:T(8,128)(2,1)} %collective-permute-done.15, bf16[1472,2048]{1,0:T(8,128)(2,1)} %collective-permute-done.14, f32[3584,2048]{1,0:T(8,128)} %fusion.1), kind=kLoop, calls=%fused_computation.19 | loop fusion | flops 18087936 | bytes 30146560 | tf_op jit(solution)/shard_map/dynamic_update_slice | solution.py:104
  670.1 20.2 %collective-permute-done.16 = bf16[288,2048]{1,0:T(8,128)(2,1)S(1)} collective-permute-done((bf16[288,2048]{1,0:T(8,128)(2,1)S(1)}, bf16[288,2048]{1,0:T(8,128)(2,1)S(1)}, u32[]{:S(2)}, u32[]{:S(2)}) %collective-permute-start.16) | collective-permute-done | bytes 1179680 | tf_op jit(solution)/shard_map/ppermute | solution.py:14
  690.3 3.6 fusion.20
  693.9 1.1 collective-permute-done.18
  695.0 1.7 fusion.24
  (45 shorter events, 0.1 us)
Async XLA Ops:
  0.6 54.2 %collective-permute-start.1 = (bf16[352,2048]{1,0:T(8,128)(2,1)}, bf16[352,2048]{1,0:T(8,128)(2,1)}, u32[]{:S(2)}, u32[]{:S(2)}) collective-permute-start(bf16[352,2048]{1,0:T(8,128)(2,1)} %bitcast.66), channel_id=1, source_target_pairs={{0,2},{2,4},{4,6},{6,0},{1,3},{3,5},{5,7},{7,1},{8,10},{10,12},{12... | collective-permute-start | bytes 4325384 | tf_op jit(solution)/shard_map/ppermute | solution.py:14
  3.6 63.8 %collective-permute-start.2 = (bf16[352,2048]{1,0:T(8,128)(2,1)}, bf16[352,2048]{1,0:T(8,128)(2,1)}, u32[]{:S(2)}, u32[]{:S(2)}) collective-permute-start(bf16[352,2048]{1,0:T(8,128)(2,1)} %bitcast.67), channel_id=1, source_target_pairs={{0,4},{2,6},{4,0},{6,2},{1,5},{3,7},{5,1},{7,3},{8,12},{10,14},{12... | collective-permute-start | bytes 4325384 | tf_op jit(solution)/shard_map/ppermute | solution.py:14
  5.2 68.7 %collective-permute-start.3 = (bf16[352,2048]{1,0:T(8,128)(2,1)}, bf16[352,2048]{1,0:T(8,128)(2,1)}, u32[]{:S(2)}, u32[]{:S(2)}) collective-permute-start(bf16[352,2048]{1,0:T(8,128)(2,1)} %bitcast.68), channel_id=1, source_target_pairs={{0,6},{2,0},{4,2},{6,4},{1,7},{3,1},{5,3},{7,5},{8,14},{10,8},{12,... | collective-permute-start | bytes 4325384 | tf_op jit(solution)/shard_map/ppermute | solution.py:14
  6.6 70.3 %collective-permute-start = (bf16[704,3584]{1,0:T(8,128)(2,1)}, bf16[704,3584]{1,0:T(8,128)(2,1)}, u32[]{:S(2)}, u32[]{:S(2)}) collective-permute-start(bf16[704,3584]{1,0:T(8,128)(2,1)} %bitcast.63), channel_id=1, source_target_pairs={{0,1},{1,0},{2,3},{3,2},{4,5},{5,4},{6,7},{7,6},{8,9},{9,8},{10,11... | collective-permute-start | bytes 15138824 | tf_op jit(solution)/shard_map/ppermute | solution.py:14
  8.4 132.2 %collective-permute-start.9 = (bf16[64,2048]{1,0:T(8,128)(2,1)}, bf16[64,2048]{1,0:T(8,128)(2,1)}, u32[]{:S(2)}, u32[]{:S(2)}) collective-permute-start(bf16[64,2048]{1,0:T(8,128)(2,1)} %fusion.21), channel_id=1, source_target_pairs={{0,24},{8,0},{16,8},{24,16},{1,25},{9,1},{17,9},{25,17},{2,26},{10... | collective-permute-start | bytes 786440 | tf_op jit(solution)/shard_map/ppermute | solution.py:14
  16.2 6.5 copy-start.3
  24.0 19.6 %slice-start = ((s8[14680064]{0:T(1024)(128)(4,1)}), s8[4194304]{0:T(1024)(128)(4,1)S(1)}, s32[]{:S(2)}) async-start(s8[14680064]{0:T(1024)(128)(4,1)} %bitcast.61), calls=%async_computation | async-start | bytes 8388608
  24.0 19.6 %slice-start.1 = ((s8[14680064]{0:T(1024)(128)(4,1)}), s8[2097152]{0:T(1024)(128)(4,1)S(1)}, s32[]{:S(2)}) async-start(s8[14680064]{0:T(1024)(128)(4,1)} %bitcast.61), calls=%async_computation.1 | async-start | bytes 4194304
  33.6 10.0 %slice-start.2 = ((s8[14680064]{0:T(1024)(128)(4,1)}), s8[4194304]{0:T(1024)(128)(4,1)S(1)}, s32[]{:S(2)}) async-start(s8[14680064]{0:T(1024)(128)(4,1)} %bitcast.61), calls=%async_computation.2 | async-start | bytes 8388608
  33.6 10.0 %slice-start.3 = ((s8[14680064]{0:T(1024)(128)(4,1)}), s8[4194304]{0:T(1024)(128)(4,1)S(1)}, s32[]{:S(2)}) async-start(s8[14680064]{0:T(1024)(128)(4,1)} %bitcast.61), calls=%async_computation.3 | async-start | bytes 8388608
  54.8 87.4 %collective-permute-start.8 = (bf16[64,2048]{1,0:T(8,128)(2,1)}, bf16[64,2048]{1,0:T(8,128)(2,1)S(1)}, u32[]{:S(2)}, u32[]{:S(2)}) collective-permute-start(bf16[64,2048]{1,0:T(8,128)(2,1)} %fusion.21), channel_id=1, source_target_pairs={{0,8},{8,16},{16,24},{24,0},{1,9},{9,17},{17,25},{25,1},{2,10},{10... | collective-permute-start | bytes 786440 | tf_op jit(solution)/shard_map/ppermute | solution.py:14
  67.4 74.8 %collective-permute-start.11 = (bf16[448,2048]{1,0:T(8,128)(2,1)}, bf16[448,2048]{1,0:T(8,128)(2,1)}, u32[]{:S(2)}, u32[]{:S(2)}) collective-permute-start(bf16[448,2048]{1,0:T(8,128)(2,1)} %fusion.15), channel_id=1, source_target_pairs={{0,24},{8,0},{16,8},{24,16},{1,25},{9,1},{17,9},{25,17},{2,26},{10... | collective-permute-start | bytes 5505032 | tf_op jit(solution)/shard_map/ppermute | solution.py:14
  73.8 568.5 %collective-permute-start.13 = (bf16[1280,2048]{1,0:T(8,128)(2,1)}, bf16[1280,2048]{1,0:T(8,128)(2,1)}, u32[]{:S(2)}, u32[]{:S(2)}) collective-permute-start(bf16[1280,2048]{1,0:T(8,128)(2,1)} %fusion.12), channel_id=1, source_target_pairs={{0,24},{8,0},{16,8},{24,16},{1,25},{9,1},{17,9},{25,17},{2,26},{10... | collective-permute-start | bytes 15728648 | tf_op jit(solution)/shard_map/ppermute | solution.py:14
  106.7 2.5 copy-start
  110.9 32.9 %collective-permute-start.6 = (bf16[352,2048]{1,0:T(8,128)(2,1)S(1)}, bf16[352,2048]{1,0:T(8,128)(2,1)S(1)}, u32[]{:S(2)}, u32[]{:S(2)}) collective-permute-start(bf16[352,2048]{1,0:T(8,128)(2,1)S(1)} %get-tuple-element.10), channel_id=1, source_target_pairs={{0,6},{2,0},{4,2},{6,4},{1,7},{3,1},{5,3},{7,5},{8,14},{10,8},{12,... | collective-permute-start | bytes 4325384 | tf_op jit(solution)/shard_map/ppermute | solution.py:14
  140.6 501.7 %collective-permute-start.12 = (bf16[1280,2048]{1,0:T(8,128)(2,1)}, bf16[1280,2048]{1,0:T(8,128)(2,1)}, u32[]{:S(2)}, u32[]{:S(2)}) collective-permute-start(bf16[1280,2048]{1,0:T(8,128)(2,1)} %fusion.12), channel_id=1, source_target_pairs={{0,8},{8,16},{16,24},{24,0},{1,9},{9,17},{17,25},{25,1},{2,10},{10... | collective-permute-start | bytes 15728648 | tf_op jit(solution)/shard_map/ppermute | solution.py:14
  142.2 2.8 copy-start.5
  142.2 67.5 %collective-permute-start.7 = (bf16[704,3584]{1,0:T(8,128)(2,1)S(1)}, bf16[704,3584]{1,0:T(8,128)(2,1)}, u32[]{:S(2)}, u32[]{:S(2)}) collective-permute-start(bf16[704,3584]{1,0:T(8,128)(2,1)S(1)} %constant_dynamic-slice_fusion), channel_id=1, source_target_pairs={{0,1},{1,0},{2,3},{3,2},{4,5},{5,4},{6,7},{7,6},{8,9},{9,8},{10,11... | collective-permute-start | bytes 15138824 | tf_op jit(solution)/shard_map/ppermute | solution.py:14
  142.2 65.2 %collective-permute-start.5 = (bf16[352,2048]{1,0:T(8,128)(2,1)}, bf16[352,2048]{1,0:T(8,128)(2,1)}, u32[]{:S(2)}, u32[]{:S(2)}) collective-permute-start(bf16[352,2048]{1,0:T(8,128)(2,1)} %get-tuple-element.11), channel_id=1, source_target_pairs={{0,4},{2,6},{4,0},{6,2},{1,5},{3,7},{5,1},{7,3},{8,12},{10,14},{12... | collective-permute-start | bytes 4325384 | tf_op jit(solution)/shard_map/ppermute | solution.py:14
  143.9 1.1 copy-start.1
  145.0 72.2 %collective-permute-start.4 = (bf16[352,2048]{1,0:T(8,128)(2,1)S(1)}, bf16[352,2048]{1,0:T(8,128)(2,1)}, u32[]{:S(2)}, u32[]{:S(2)}) collective-permute-start(bf16[352,2048]{1,0:T(8,128)(2,1)S(1)} %get-tuple-element.9), channel_id=1, source_target_pairs={{0,2},{2,4},{4,6},{6,0},{1,3},{3,5},{5,7},{7,1},{8,10},{10,12},{12... | collective-permute-start | bytes 4325384 | tf_op jit(solution)/shard_map/ppermute | solution.py:14
  188.2 29.1 %copy-start.2 = (bf16[352,2048]{1,0:T(8,128)(2,1)S(1)}, bf16[352,2048]{1,0:T(8,128)(2,1)}, u32[]{:S(2)}) copy-start(bf16[352,2048]{1,0:T(8,128)(2,1)} %copy-done.1) | copy-start | bytes 4325380
  207.4 451.5 %collective-permute-start.15 = (bf16[1472,2048]{1,0:T(8,128)(2,1)}, bf16[1472,2048]{1,0:T(8,128)(2,1)}, u32[]{:S(2)}, u32[]{:S(2)}) collective-permute-start(bf16[1472,2048]{1,0:T(8,128)(2,1)} %fusion.9), channel_id=1, source_target_pairs={{0,24},{8,0},{16,8},{24,16},{1,25},{9,1},{17,9},{25,17},{2,26},{10... | collective-permute-start | bytes 18087944 | tf_op jit(solution)/shard_map/ppermute | solution.py:14
  209.7 449.3 %collective-permute-start.14 = (bf16[1472,2048]{1,0:T(8,128)(2,1)}, bf16[1472,2048]{1,0:T(8,128)(2,1)}, u32[]{:S(2)}, u32[]{:S(2)}) collective-permute-start(bf16[1472,2048]{1,0:T(8,128)(2,1)} %fusion.9), channel_id=1, source_target_pairs={{0,8},{8,16},{16,24},{24,0},{1,9},{9,17},{17,25},{25,1},{2,10},{10... | collective-permute-start | bytes 18087944 | tf_op jit(solution)/shard_map/ppermute | solution.py:14
  217.2 4.5 copy-start.6
  217.2 417.0 %collective-permute-start.10 = (bf16[448,2048]{1,0:T(8,128)(2,1)}, bf16[448,2048]{1,0:T(8,128)(2,1)S(1)}, u32[]{:S(2)}, u32[]{:S(2)}) collective-permute-start(bf16[448,2048]{1,0:T(8,128)(2,1)} %fusion.15), channel_id=1, source_target_pairs={{0,8},{8,16},{16,24},{24,0},{1,9},{9,17},{17,25},{25,1},{2,10},{10... | collective-permute-start | bytes 5505032 | tf_op jit(solution)/shard_map/ppermute | solution.py:14
  222.9 411.3 %copy-start.4 = (bf16[288,2048]{1,0:T(8,128)(2,1)S(1)}, bf16[288,2048]{1,0:T(8,128)(2,1)}, u32[]{:S(2)}) copy-start(bf16[288,2048]{1,0:T(8,128)(2,1)} %fusion.18) | copy-start | bytes 3538948
  230.3 412.0 %copy-start.7 = (bf16[32,2048]{1,0:T(8,128)(2,1)S(1)}, bf16[32,2048]{1,0:T(8,128)(2,1)}, u32[]{:S(2)}) copy-start(bf16[32,2048]{1,0:T(8,128)(2,1)} %fusion.22) | copy-start | bytes 393220
  634.3 35.9 %collective-permute-start.17 = (bf16[288,2048]{1,0:T(8,128)(2,1)S(1)}, bf16[288,2048]{1,0:T(8,128)(2,1)}, u32[]{:S(2)}, u32[]{:S(2)}) collective-permute-start(bf16[288,2048]{1,0:T(8,128)(2,1)S(1)} %copy-done.4), channel_id=1, source_target_pairs={{0,24},{8,0},{16,8},{24,16},{1,25},{9,1},{17,9},{25,17},{2,26},{10... | collective-permute-start | bytes 3538952 | tf_op jit(solution)/shard_map/ppermute | solution.py:14
  642.3 48.0 %collective-permute-start.16 = (bf16[288,2048]{1,0:T(8,128)(2,1)S(1)}, bf16[288,2048]{1,0:T(8,128)(2,1)S(1)}, u32[]{:S(2)}, u32[]{:S(2)}) collective-permute-start(bf16[288,2048]{1,0:T(8,128)(2,1)S(1)} %copy-done.4), channel_id=1, source_target_pairs={{0,8},{8,16},{16,24},{24,0},{1,9},{9,17},{17,25},{25,1},{2,10},{10... | collective-permute-start | bytes 3538952 | tf_op jit(solution)/shard_map/ppermute | solution.py:14
  642.3 51.6 %collective-permute-start.19 = (bf16[32,2048]{1,0:T(8,128)(2,1)S(1)}, bf16[32,2048]{1,0:T(8,128)(2,1)S(1)}, u32[]{:S(2)}, u32[]{:S(2)}) collective-permute-start(bf16[32,2048]{1,0:T(8,128)(2,1)S(1)} %copy-done.7), channel_id=1, source_target_pairs={{0,24},{8,0},{16,8},{24,16},{1,25},{9,1},{17,9},{25,17},{2,26},{10... | collective-permute-start | bytes 393224 | tf_op jit(solution)/shard_map/ppermute | solution.py:14
  659.0 36.0 %collective-permute-start.18 = (bf16[32,2048]{1,0:T(8,128)(2,1)S(1)}, bf16[32,2048]{1,0:T(8,128)(2,1)S(1)}, u32[]{:S(2)}, u32[]{:S(2)}) collective-permute-start(bf16[32,2048]{1,0:T(8,128)(2,1)S(1)} %copy-done.7), channel_id=1, source_target_pairs={{0,8},{8,16},{16,24},{24,0},{1,9},{9,17},{17,25},{25,1},{2,10},{10... | collective-permute-start | bytes 393224 | tf_op jit(solution)/shard_map/ppermute | solution.py:14
